TPU v7x, 32 devices: a whole 2x2x4 slice. The times are simulated.
32 devices in a mesh: dp: 8 (over z, x), tensor: 4 (over y, core).
Axes of the slice: x: 2, y: 2, z: 4, core: 2. Of those that a mesh axis runs over, the one named last changes fastest.
Arguments:
- queries: bfloat16 [256, 32, 2048], P('dp', None, 'tensor'), may hold values from -8 to 8
- keys: bfloat16 [256, 32, 512], P('dp', None, 'tensor'), may hold values from -8 to 8
- values: bfloat16 [256, 32, 512], P('dp', None, 'tensor'), may hold values from -6 to 6
- out_weight: bfloat16 [2048, 4096], P(None, 'tensor'), may hold values from -0.125 to 0.125
- dest_slot: int32 [256], P('dp'), may hold values from 0 to 31, as said below
- pack_slot: int32 [8, 32], P('dp'), may hold values from 0 to 31, as said below
- seq_start: int32 [8, 32], P('dp'), may hold values from 0 to 1024, as said below
- seq_len: int32 [8, 32], P('dp'), may hold values from 0 to 1024, as said below
Outputs:
- projected: bfloat16 [256, 32, 4096], P('dp', None, 'tensor')
Inputs may be any that keep to these rules, and one draw needn't show every extreme that they name: Block i of loader l goes to pack dest_slot[l * 32 + i] // 4; the 32 values of one loader are distinct. pack_slot[p, s] = l * 4 + m names the block of loader l whose dest_slot is p * 4 + m; the values of one pack are distinct, and every block of every loader fills exactly one position of one pack, so each pack holds exactly 32 blocks. Multiples of 32; seq_start[p, 0] = 0, the used entries rise, and a sequence's blocks run up to the next used start (or to the pack's end); the entries after the used ones equal 1024. Some pack holds a single sequence of all its blocks. `seq_len`: for a used sequence of b blocks, from b * 32 - 32 // 4 + 1 to b * 32; 0 for unused entries.
All inputs are finite; a program needn't handle non-finite values.
Results may differ from a plain program's by a relative error of at most 0.01.
Values may be sent and summed in bfloat16 or wider, within the bound.
No kernel may reach another device: no remote copies, remote signals or barrier semaphores. Data moves between devices by JAX's collectives and lax.ppermute only.
A program may use at most 64 MiB of HBM per device.

v0:
```python
import jax
import jax.numpy as jnp
from jax import lax
from jax.sharding import PartitionSpec as P

HEAD_SIZE = 128


def tile_scores(query_tile, key_tile, score_scale):
    return (
        jnp.einsum("rgnd,cgd->gnrc", query_tile, key_tile, preferred_element_type=jnp.float32)
        * score_scale
    )


def tile_mix(weight_tile, value_tile):
    return jnp.einsum("gnrc,cgd->rgnd", weight_tile, value_tile, preferred_element_type=jnp.float32)


def attend(packed_queries, packed_keys, packed_values, starts, lengths, block_rows):
    total_row_count, query_cols = packed_queries.shape
    kv_heads = packed_keys.shape[1] // HEAD_SIZE
    query_group_count = query_cols // HEAD_SIZE // kv_heads
    tile_rows = 16 * block_rows
    score_scale = 1.0 / HEAD_SIZE**0.5
    row_ids = jnp.arange(total_row_count, dtype=jnp.int32)
    segment = jnp.sum((starts[None, :] <= row_ids[:, None]).astype(jnp.int32), axis=1) - 1
    picked = segment[:, None] == jnp.arange(starts.shape[0], dtype=jnp.int32)[None, :]
    begins = jnp.sum(jnp.where(picked, starts[None, :], 0), axis=1)
    limits = jnp.sum(jnp.where(picked, lengths[None, :], 0), axis=1)
    usable = row_ids - begins < limits
    query_head_rows = packed_queries.reshape(
        total_row_count, kv_heads, query_group_count, HEAD_SIZE
    )
    key_head_rows = packed_keys.reshape(total_row_count, kv_heads, HEAD_SIZE)
    value_head_rows = packed_values.reshape(total_row_count, kv_heads, HEAD_SIZE)
    blocks_out = []
    for tile_index in range(total_row_count // tile_rows):
        first_row = tile_index * tile_rows
        end_row = first_row + tile_rows
        query_tile = query_head_rows[first_row:end_row]
        score_tiles = []
        needed_flags = []
        for key_index in range(tile_index + 1):
            key_first = key_index * tile_rows
            key_tile = key_head_rows[key_first : key_first + tile_rows]
            needed = jnp.array(True)
            scores = tile_scores(query_tile, key_tile, score_scale)
            score_tiles.append(scores)
            needed_flags.append(needed)
        scores = jnp.concatenate(score_tiles, axis=-1)
        allowed = (segment[first_row:end_row, None] == segment[None, :end_row]) & (
            row_ids[None, :end_row] <= row_ids[first_row:end_row, None]
        )
        scores = jnp.where(allowed[None, None], scores, -jnp.inf)
        largest = jnp.max(scores, axis=-1, keepdims=True)
        exponent = jnp.exp(scores - largest)
        weights = (exponent / jnp.sum(exponent, axis=-1, keepdims=True)).astype(jnp.bfloat16)
        mixture = jnp.zeros((tile_rows, kv_heads, query_group_count, HEAD_SIZE), jnp.float32)
        for key_index in range(tile_index + 1):
            key_first = key_index * tile_rows
            weight_tile = weights[..., key_first : key_first + tile_rows]
            value_tile = value_head_rows[key_first : key_first + tile_rows]
            part_sum = tile_mix(weight_tile, value_tile)
            mixture = mixture + part_sum
        mixture = jnp.where(usable[first_row:end_row, None, None, None], mixture, 0.0)
        blocks_out.append(mixture.reshape(tile_rows, query_cols).astype(jnp.bfloat16))
    return jnp.concatenate(blocks_out, axis=0)


def body(queries, keys, values, out_weight, dest_slot, pack_slot, seq_start, seq_len):
    local_blocks, block_rows, query_cols = queries.shape
    loaders = lax.axis_size("dp")
    capacity = (local_blocks + loaders - 1) // loaders
    slot_count = loaders * capacity

    def outgoing(portion):
        return (
            jnp.zeros((slot_count,) + portion.shape[1:], portion.dtype).at[dest_slot].set(portion)
        )

    arrived = (
        lax.all_to_all(outgoing(queries), "dp", split_axis=0, concat_axis=0, tiled=True),
        lax.all_to_all(outgoing(keys), "dp", split_axis=0, concat_axis=0, tiled=True),
        lax.all_to_all(outgoing(values), "dp", split_axis=0, concat_axis=0, tiled=True),
    )
    sources = pack_slot[0]

    def collect(portion):
        return jnp.take(portion, sources, axis=0).reshape(
            local_blocks * block_rows, portion.shape[2]
        )

    attended = attend(
        collect(arrived[0]),
        collect(arrived[1]),
        collect(arrived[2]),
        seq_start[0],
        seq_len[0],
        block_rows,
    )
    going_back = (
        jnp.zeros((slot_count, block_rows, query_cols), jnp.bfloat16)
        .at[sources]
        .set(attended.reshape(local_blocks, block_rows, query_cols))
    )
    returned = lax.all_to_all(going_back, "dp", split_axis=0, concat_axis=0, tiled=True)
    own_rows = jnp.take(returned, dest_slot, axis=0).reshape(local_blocks * block_rows, query_cols)
    projected = jnp.dot(
        lax.all_gather(own_rows, "tensor", axis=1, tiled=True),
        out_weight,
        preferred_element_type=jnp.float32,
    )
    return projected.astype(jnp.bfloat16).reshape(local_blocks, block_rows, out_weight.shape[1])


def solution(mesh):
    placed = (
        P("dp", None, "tensor"),
        P("dp", None, "tensor"),
        P("dp", None, "tensor"),
        P(None, "tensor"),
        P("dp"),
        P("dp", None),
        P("dp", None),
        P("dp", None),
    )
    return jax.shard_map(
        body, mesh=mesh, in_specs=placed, out_specs=P("dp", None, "tensor"), check_vma=False
    )
```

profile of v0, /device:TPU:0, one launch (start us, length us, event | category | flops | bytes accessed | tf_op | source)
XLA Modules:
  0.0 168.2 jit_solution(10678091339216398935)
XLA Ops:
  6.5 0.7 compare_select_fusion
  7.3 0.7 broadcast.202.clone.1
  8.0 4.3 %scatter_fusion = bf16[32,32,128]{2,1,0:T(8,128)(2,1)} fusion(bf16[32,32,128]{2,1,0:T(8,128)(2,1)} %broadcast.202.clone.1, s32[32]{0:T(128)S(1)} %compare_select_fusion, bf16[32,32,128]{2,1,0:T(8,128)(2,1)} %param.14), kind=kCustom, calls=%fused_computation.4 | custom fusion | bytes 786560 | tf_op jit(solution)/shard_map/scatter | solution.py:79
  12.3 7.3 %all-to-all-start = ((bf16[32,32,128]{2,1,0:T(8,128)(2,1)}), bf16[32,32,128]{2,1,0:T(8,128)(2,1)S(1)}, u32[]{:S(2)}, u32[]{:S(2)}) async-start(bf16[32,32,128]{2,1,0:T(8,128)(2,1)} %scatter_fusion), calls=%async_computation | async-start | bytes 524288 | tf_op jit(solution)/shard_map/all_to_all | solution.py:85
  19.6 0.7 broadcast.202.clone
  20.3 4.3 %scatter_fusion.1 = bf16[32,32,128]{2,1,0:T(8,128)(2,1)} fusion(bf16[32,32,128]{2,1,0:T(8,128)(2,1)} %broadcast.202.clone, s32[32]{0:T(128)S(1)} %compare_select_fusion, bf16[32,32,128]{2,1,0:T(8,128)(2,1)} %param.13), kind=kCustom, calls=%fused_computation.5 | custom fusion | bytes 786560 | tf_op jit(solution)/shard_map/scatter | solution.py:79
  24.6 0.7 convert_reduce_fusion
  25.3 3.2 %all-to-all-done = bf16[32,32,128]{2,1,0:T(8,128)(2,1)S(1)} async-done(((bf16[32,32,128]{2,1,0:T(8,128)(2,1)}), bf16[32,32,128]{2,1,0:T(8,128)(2,1)S(1)}, u32[]{:S(2)}, u32[]{:S(2)}) %all-to-all-start) | async-done | bytes 262176 | tf_op jit(solution)/shard_map/all_to_all | solution.py:85
  28.5 3.6 %all-to-all-start.1 = ((bf16[32,32,128]{2,1,0:T(8,128)(2,1)}), bf16[32,32,128]{2,1,0:T(8,128)(2,1)S(1)}, u32[]{:S(2)}, u32[]{:S(2)}) async-start(bf16[32,32,128]{2,1,0:T(8,128)(2,1)} %scatter_fusion.1), calls=%async_computation.1 | async-start | bytes 524288 | tf_op jit(solution)/shard_map/all_to_all | solution.py:84
  32.1 0.7 compare_select_fusion.1
  32.8 1.1 broadcast.198.clone
  33.9 4.6 %scatter_fusion.2 = bf16[32,32,512]{2,1,0:T(8,128)(2,1)} fusion(bf16[32,32,512]{2,1,0:T(8,128)(2,1)} %broadcast.198.clone, s32[32]{0:T(128)S(1)} %compare_select_fusion, bf16[32,32,512]{2,1,0:T(8,128)(2,1)S(1)} %copy-done), kind=kCustom, calls=%fused_computation.6 | custom fusion | bytes 3145856 | tf_op jit(solution)/shard_map/scatter | solution.py:79
  38.5 0.1 select_reduce_fusion.1
  38.6 2.1 %all-to-all-done.1 = bf16[32,32,128]{2,1,0:T(8,128)(2,1)S(1)} async-done(((bf16[32,32,128]{2,1,0:T(8,128)(2,1)}), bf16[32,32,128]{2,1,0:T(8,128)(2,1)S(1)}, u32[]{:S(2)}, u32[]{:S(2)}) %all-to-all-start.1) | async-done | bytes 262176 | tf_op jit(solution)/shard_map/all_to_all | solution.py:84
  40.7 3.9 %all-to-all-start.2 = ((bf16[32,32,512]{2,1,0:T(8,128)(2,1)}), bf16[32,32,512]{2,1,0:T(8,128)(2,1)S(1)}, u32[]{:S(2)}, u32[]{:S(2)}) async-start(bf16[32,32,512]{2,1,0:T(8,128)(2,1)} %scatter_fusion.2), calls=%async_computation.2 | async-start | bytes 2097152 | tf_op jit(solution)/shard_map/all_to_all | solution.py:83
  44.7 0.3 compare_and_fusion
  44.9 0.5 fusion.8
  45.4 0.6 gather_fusion
  46.0 0.6 gather_fusion.1
  46.6 0.1 broadcast_select_fusion.2
  46.8 23.0 %all-to-all-done.2 = bf16[32,32,512]{2,1,0:T(8,128)(2,1)S(1)} async-done(((bf16[32,32,512]{2,1,0:T(8,128)(2,1)}), bf16[32,32,512]{2,1,0:T(8,128)(2,1)S(1)}, u32[]{:S(2)}, u32[]{:S(2)}) %all-to-all-start.2) | async-done | bytes 1048608 | tf_op jit(solution)/shard_map/all_to_all | solution.py:83
  69.8 0.6 gather_fusion.2
  70.4 0.2 broadcast_select_fusion.1
  70.6 0.1 fusion.30
  70.7 0.1 reshape.323
  70.8 0.9 fusion.3
  71.7 0.9 fusion.2
  72.6 1.4 fusion.18
  74.1 0.2 copy.32
  74.3 0.1 reshape.325
  74.4 0.7 multiply_bitcast_fusion.1
  75.1 0.7 multiply_bitcast_fusion
  75.9 1.2 fusion.1
  77.1 1.6 fusion
  78.6 1.7 %divide_convert_fusion = bf16[1,4,512,1024]{2,3,1,0:T(8,128)(2,1)S(1)} fusion(f32[1,4,512,512]{2,3,1,0:T(8,128)S(1)} %multiply_bitcast_fusion, f32[1,4,512,512]{2,3,1,0:T(8,128)S(1)} %multiply_bitcast_fusion.1, f32[4,512]{1,0:T(4,128)S(1)} %fusion, f32[4,512]{1,0:T(4,128)S(1)} %fusion.1, pred[512,1024]{0,1:T(8,128)(4,1)S(1)} %fusion.8), kind=kLoop, calls=%fused_computation.9 | loop fusion | flops 10485760 | bytes 13123584 | tf_op jit(solution)/shard_map/convert_element_type | solution.py:58
  80.4 0.5 fusion.4
  80.9 0.5 fusion.22
  81.3 0.2 copy.33
  81.6 0.1 pad_maximum_fusion
  81.7 1.1 broadcast.198
  82.7 4.6 %scatter_fusion.3 = bf16[32,32,512]{2,1,0:T(8,128)(2,1)} fusion(bf16[32,32,512]{2,1,0:T(8,128)(2,1)} %broadcast.198, s32[32]{0:T(128)S(1)} %fusion.27, bf16[32,32,512]{2,1,0:T(8,128)(2,1)S(1)} %bitcast.103), kind=kCustom, calls=%fused_computation.7 | custom fusion | bytes 3145856 | tf_op jit(solution)/shard_map/scatter | solution.py:105
  87.3 3.6 %all-to-all-start.3 = ((bf16[32,32,512]{2,1,0:T(8,128)(2,1)}), bf16[32,32,512]{2,1,0:T(8,128)(2,1)S(1)}, u32[]{:S(2)}, u32[]{:S(2)}) async-start(bf16[32,32,512]{2,1,0:T(8,128)(2,1)} %scatter_fusion.3), calls=%async_computation.3 | async-start | bytes 2097152 | tf_op jit(solution)/shard_map/all_to_all | solution.py:107
  90.9 0.3 all-gather.2.cloned.1.call-start
  91.2 25.5 %all-to-all-done.3 = bf16[32,32,512]{2,1,0:T(8,128)(2,1)S(1)} async-done(((bf16[32,32,512]{2,1,0:T(8,128)(2,1)}), bf16[32,32,512]{2,1,0:T(8,128)(2,1)S(1)}, u32[]{:S(2)}, u32[]{:S(2)}) %all-to-all-start.3) | async-done | bytes 1048608 | tf_op jit(solution)/shard_map/all_to_all | solution.py:107
  116.6 0.6 gather_fusion.3
  117.3 1.1 broadcast_select_fusion
  118.4 33.7 %all-gather.2.cloned.1.call-done = bf16[1024,2048]{1,0:T(8,128)(2,1)} async-done(((bf16[1024,512]{1,0:T(8,128)(2,1)}), bf16[1024,2048]{1,0:T(8,128)(2,1)}) %all-gather.2.cloned.1.call-update) | async-done | bytes 4194320 | tf_op jit(solution)/shard_map/all_gather | solution.py:110
  152.1 9.3 %convolution_convert_fusion = bf16[1024,1024]{1,0:T(8,128)(2,1)} fusion(bf16[1024,2048]{1,0:T(8,128)(2,1)} %all-gather.2.cloned.1.call-done, bf16[2048,1024]{1,0:T(8,128)(2,1)} %param.15), kind=kOutput, calls=%fused_computation.29 | convolution fusion | flops 4296015872 | bytes 10485760 | tf_op jit(solution)/shard_map/dot_general | solution.py:109
  (25 shorter events, 0.1 us)
Async XLA Ops:
  6.5 31.9 %copy-start.1 = (s32[1,32]{1,0:T(1,128)S(1)}, s32[1,32]{1,0:T(1,128)}, u32[]{:S(2)}) copy-start(s32[1,32]{1,0:T(1,128)} %param.18) | copy-start | bytes 388
  6.5 32.0 %copy-start.3 = (s32[1,32]{1,0:T(1,128)S(1)}, s32[1,32]{1,0:T(1,128)}, u32[]{:S(2)}) copy-start(s32[1,32]{1,0:T(1,128)} %param.17) | copy-start | bytes 388
  6.5 27.3 %copy-start = (bf16[32,32,512]{2,1,0:T(8,128)(2,1)S(1)}, bf16[32,32,512]{2,1,0:T(8,128)(2,1)}, u32[]{:S(2)}) copy-start(bf16[32,32,512]{2,1,0:T(8,128)(2,1)} %param.12) | copy-start | bytes 3145732
  6.5 31.9 %copy-start.2 = (s32[1,32]{1,0:T(1,128)S(1)}, s32[1,32]{1,0:T(1,128)}, u32[]{:S(2)}) copy-start(s32[1,32]{1,0:T(1,128)} %param.19) | copy-start | bytes 388
  12.3 16.2 %all-to-all-start = ((bf16[32,32,128]{2,1,0:T(8,128)(2,1)}), bf16[32,32,128]{2,1,0:T(8,128)(2,1)S(1)}, u32[]{:S(2)}, u32[]{:S(2)}) async-start(bf16[32,32,128]{2,1,0:T(8,128)(2,1)} %scatter_fusion), calls=%async_computation | async-start | bytes 524288 | tf_op jit(solution)/shard_map/all_to_all | solution.py:85
  28.5 12.2 %all-to-all-start.1 = ((bf16[32,32,128]{2,1,0:T(8,128)(2,1)}), bf16[32,32,128]{2,1,0:T(8,128)(2,1)S(1)}, u32[]{:S(2)}, u32[]{:S(2)}) async-start(bf16[32,32,128]{2,1,0:T(8,128)(2,1)} %scatter_fusion.1), calls=%async_computation.1 | async-start | bytes 524288 | tf_op jit(solution)/shard_map/all_to_all | solution.py:84
  40.7 29.2 %all-to-all-start.2 = ((bf16[32,32,512]{2,1,0:T(8,128)(2,1)}), bf16[32,32,512]{2,1,0:T(8,128)(2,1)S(1)}, u32[]{:S(2)}, u32[]{:S(2)}) async-start(bf16[32,32,512]{2,1,0:T(8,128)(2,1)} %scatter_fusion.2), calls=%async_computation.2 | async-start | bytes 2097152 | tf_op jit(solution)/shard_map/all_to_all | solution.py:83
  81.6 9.6 %copy-start.4 = (s32[32]{0:T(128)S(1)}, s32[32]{0:T(128)}, u32[]{:S(2)}) copy-start(s32[32]{0:T(128)} %param.16) | copy-start | bytes 388
  87.3 29.3 %all-to-all-start.3 = ((bf16[32,32,512]{2,1,0:T(8,128)(2,1)}), bf16[32,32,512]{2,1,0:T(8,128)(2,1)S(1)}, u32[]{:S(2)}, u32[]{:S(2)}) async-start(bf16[32,32,512]{2,1,0:T(8,128)(2,1)} %scatter_fusion.3), calls=%async_computation.3 | async-start | bytes 2097152 | tf_op jit(solution)/shard_map/all_to_all | solution.py:107
  90.9 61.2 %all-gather.2.cloned.1.call-start = ((), (), s32[]{:S(2)}) async-start(), calls=%async_computation.4 | async-start | bytes 5242880 | tf_op jit(solution)/shard_map/all_gather | solution.py:110
Sparse Core Ops, SparseCore 0:
  118.5 33.5 all-gather.1
where the time goes:
time: 169 us; the launch traced here: 168 us
  waiting for transfers between devices  87.4 us (52%)
  local copies, waits for them, and re-layouts  24.6 us (15%)
  starting transfers between devices  18.6 us (11%)
  matrix products  14 us (8%)
  between operations  13.7 us (8%)
  other arithmetic  9.95 us (6%)
    all_gather x1, waiting for transfers between devices, body(): lax.all_gather(own_rows, 'tensor', axis=1, tiled=True)  33.7 us
    all_to_all x1, waiting for transfers between devices, body(): lax.all_to_all(going_back, 'dp', split_axis=0, concat_axis=0, tiled=True)  25.5 us
    all_to_all x1, waiting for transfers between devices, body(): lax.all_to_all(outgoing(queries), 'dp', split_axis=0, concat_axis=0, tile...  23 us
    scatter x3, local copies, waits for them, and re-layouts, outgoing(): jnp.zeros((slot_count,) + portion.shape[1:], portion.dtype).at[dest_slot]  13.1 us
    dot_general x1, matrix products, body(): jnp.dot(lax.all_gather(own_rows, 'tensor', axis=1, tiled=True), out_weigh...  9.27 us
    all_to_all x1, starting transfers between devices, body(): lax.all_to_all(outgoing(values), 'dp', split_axis=0, concat_axis=0, tiled...  7.28 us
    scatter x1, local copies, waits for them, and re-layouts, body(): going_back = jnp.zeros((slot_count, block_rows, query_cols), jnp.bfloat16...  4.57 us
    all_to_all x1, starting transfers between devices, body(): lax.all_to_all(outgoing(queries), 'dp', split_axis=0, concat_axis=0, tile...  3.95 us
  transfers between devices with their start and end apart: 5, of which 5 were waited for; matrix products, arithmetic and copies ran while one was open for 9% of the time, Pallas kernels for 0%

commit v1 on v0

--- a/solution.py
+++ b/solution.py
@@ -1,9 +1,16 @@
+import functools
+
 import jax
 import jax.numpy as jnp
 from jax import lax
+from jax.experimental import pallas as pl
+from jax.experimental.pallas import tpu as pltpu
 from jax.sharding import PartitionSpec as P
 
+
 HEAD_SIZE = 128
+MASKED = -1e30
+SHARES = (3, 3, 2)
 
 
 def tile_scores(query_tile, key_tile, score_scale):
@@ -38,17 +45,9 @@
     for tile_index in range(total_row_count // tile_rows):
         first_row = tile_index * tile_rows
         end_row = first_row + tile_rows
-        query_tile = query_head_rows[first_row:end_row]
-        score_tiles = []
-        needed_flags = []
-        for key_index in range(tile_index + 1):
-            key_first = key_index * tile_rows
-            key_tile = key_head_rows[key_first : key_first + tile_rows]
-            needed = jnp.array(True)
-            scores = tile_scores(query_tile, key_tile, score_scale)
-            score_tiles.append(scores)
-            needed_flags.append(needed)
-        scores = jnp.concatenate(score_tiles, axis=-1)
+        scores = tile_scores(
+            query_head_rows[first_row:end_row], key_head_rows[:end_row], score_scale
+        )
         allowed = (segment[first_row:end_row, None] == segment[None, :end_row]) & (
             row_ids[None, :end_row] <= row_ids[first_row:end_row, None]
         )
@@ -56,19 +55,15 @@
         largest = jnp.max(scores, axis=-1, keepdims=True)
         exponent = jnp.exp(scores - largest)
         weights = (exponent / jnp.sum(exponent, axis=-1, keepdims=True)).astype(jnp.bfloat16)
-        mixture = jnp.zeros((tile_rows, kv_heads, query_group_count, HEAD_SIZE), jnp.float32)
-        for key_index in range(tile_index + 1):
-            key_first = key_index * tile_rows
-            weight_tile = weights[..., key_first : key_first + tile_rows]
-            value_tile = value_head_rows[key_first : key_first + tile_rows]
-            part_sum = tile_mix(weight_tile, value_tile)
-            mixture = mixture + part_sum
+        mixture = tile_mix(weights, value_head_rows[:end_row])
         mixture = jnp.where(usable[first_row:end_row, None, None, None], mixture, 0.0)
         blocks_out.append(mixture.reshape(tile_rows, query_cols).astype(jnp.bfloat16))
     return jnp.concatenate(blocks_out, axis=0)
 
 
-def body(queries, keys, values, out_weight, dest_slot, pack_slot, seq_start, seq_len):
+def exchange_body(
+    queries, keys, values, out_weight, dest_slot, pack_slot, seq_start, seq_len
+):
     local_blocks, block_rows, query_cols = queries.shape
     loaders = lax.axis_size("dp")
     capacity = (local_blocks + loaders - 1) // loaders
@@ -79,10 +74,9 @@
             jnp.zeros((slot_count,) + portion.shape[1:], portion.dtype).at[dest_slot].set(portion)
         )
 
-    arrived = (
-        lax.all_to_all(outgoing(queries), "dp", split_axis=0, concat_axis=0, tiled=True),
-        lax.all_to_all(outgoing(keys), "dp", split_axis=0, concat_axis=0, tiled=True),
-        lax.all_to_all(outgoing(values), "dp", split_axis=0, concat_axis=0, tiled=True),
+    arrived = tuple(
+        lax.all_to_all(outgoing(portion), "dp", split_axis=0, concat_axis=0, tiled=True)
+        for portion in (queries, keys, values)
     )
     sources = pack_slot[0]
 
@@ -112,6 +106,339 @@
         preferred_element_type=jnp.float32,
     )
     return projected.astype(jnp.bfloat16).reshape(local_blocks, block_rows, out_weight.shape[1])
+
+
+VMEM = pl.BlockSpec(memory_space=pltpu.VMEM)
+SMEM = pl.BlockSpec(memory_space=pltpu.SMEM)
+HBM = pl.BlockSpec(memory_space=pltpu.HBM)
+ROOM = pltpu.CompilerParams(vmem_limit_bytes=24 * 2**20)
+
+
+def sort_kernel(slots_ref, key_ref, value_ref, inverse_ref, whole_ref, *part_refs):
+    blocks = key_ref.shape[0]
+
+    def note(index, carry):
+        inverse_ref[slots_ref[index]] = index
+        return carry
+
+    lax.fori_loop(0, blocks, note, 0, unroll=4)
+    slot = 0
+    for part_ref in part_refs:
+        for index in range(part_ref.shape[0]):
+            source = inverse_ref[slot]
+            both = jnp.concatenate([key_ref[source], value_ref[source]], axis=-1)
+            part_ref[index] = both
+            whole_ref[slot] = both
+            slot += 1
+
+
+def sort_blocks(keys, values, dest_slot, parts):
+    blocks, rows, cols = keys.shape
+    shapes = [(blocks, rows, 2 * cols)] + [(part, rows, 2 * cols) for part in parts]
+    return pl.pallas_call(
+        sort_kernel,
+        out_shape=[jax.ShapeDtypeStruct((blocks,), jnp.int32)]
+        + [jax.ShapeDtypeStruct(shape, keys.dtype) for shape in shapes],
+        in_specs=[SMEM, VMEM, VMEM],
+        out_specs=[SMEM] + [VMEM] * len(shapes),
+        compiler_params=ROOM,
+        name="sort_blocks",
+    )(dest_slot, keys, values)
+
+
+def plan_kernel(
+    block_rows, capacity, tables_ref, place_ref, position_ref, query_ref, low_ref, limit_ref
+):
+    blocks = query_ref.shape[0] // 3
+    packs = position_ref.shape[0] // blocks
+    own = place_ref[0] * capacity
+
+    def one_pack(pack, carry):
+        base = pack * 3 * blocks
+        begin = tables_ref[base + blocks]
+        limit = begin + tables_ref[base + 2 * blocks]
+        after = 1
+        for position in range(blocks):
+            position_ref[pack * blocks + tables_ref[base + position]] = position
+            if position > 0:
+                upcoming = tables_ref[base + blocks + after]
+                reached = upcoming <= position * block_rows
+                begin = jnp.where(reached, upcoming, begin)
+                limit = jnp.where(
+                    reached, upcoming + tables_ref[base + 2 * blocks + after], limit
+                )
+                after = jnp.minimum(jnp.where(reached, after + 1, after), blocks - 1)
+            low_ref[position] = begin
+            limit_ref[position] = limit
+        for member in range(capacity):
+            position = position_ref[pack * blocks + own + member]
+            query_ref[pack * capacity + member] = position * block_rows
+            query_ref[blocks + pack * capacity + member] = low_ref[position]
+            query_ref[2 * blocks + pack * capacity + member] = limit_ref[position]
+        return carry
+
+    lax.fori_loop(0, packs, one_pack, 0)
+
+
+def plan(tables, place, blocks, block_rows, capacity):
+    return pl.pallas_call(
+        functools.partial(plan_kernel, block_rows, capacity),
+        out_shape=[
+            jax.ShapeDtypeStruct((tables.shape[0] // 3,), jnp.int32),
+            jax.ShapeDtypeStruct((3 * blocks,), jnp.int32),
+        ],
+        in_specs=[SMEM, SMEM],
+        out_specs=[SMEM, SMEM],
+        scratch_shapes=[pltpu.SMEM((blocks,), jnp.int32)] * 2,
+        compiler_params=ROOM,
+        name="plan",
+    )(tables, place)
+
+
+def attend_kernel(
+    first, capacity, masks, offsets, position_ref, info_ref, inverse_ref, place_ref, query_ref, *refs
+):
+    sources = len(masks)
+    item_refs = refs[:sources]
+    out_ref, staged_ref, key_ref, value_ref, semaphores = refs[sources:]
+    count, block_rows, query_cols = staged_ref.shape
+    total = key_ref.shape[0]
+    blocks = total // block_rows
+    heads = query_cols // HEAD_SIZE
+    place = place_ref[0]
+    scale = 1.4426950408889634 / HEAD_SIZE**0.5
+    copies = []
+    for pack in range(count // capacity):
+        table = (first + pack) * blocks
+        for index, mask in enumerate(masks):
+            origin = table + jnp.bitwise_xor(place, mask) * capacity
+            for member in range(capacity):
+                begin = pl.multiple_of(position_ref[origin + member] * block_rows, block_rows)
+                rows = pl.ds(begin, block_rows)
+                block = item_refs[index][offsets[index] + pack * capacity + member]
+                key_ref[rows, :] = block[:, :HEAD_SIZE]
+                value_ref[rows, :] = block[:, HEAD_SIZE:]
+        stacks = []
+        for member in range(capacity):
+            index = pack * capacity + member
+            query = query_ref[inverse_ref[first * capacity + index]]
+            stacks += [query[:, head * HEAD_SIZE : (head + 1) * HEAD_SIZE] for head in range(heads)]
+        scores = lax.dot_general(
+            jnp.concatenate(stacks, axis=0),
+            key_ref[...],
+            (((1,), (1,)), ((), ())),
+            preferred_element_type=jnp.float32,
+        )
+        masses = []
+        weights = []
+        for member in range(capacity):
+            index = pack * capacity + member
+            row_base = info_ref[first * capacity + index]
+            low = info_ref[blocks + first * capacity + index]
+            column = lax.broadcasted_iota(jnp.int32, (block_rows, total), 1)
+            row = lax.broadcasted_iota(jnp.int32, (block_rows, total), 0) + row_base
+            allowed = (column <= row) & (column >= low)
+            for head in range(heads):
+                begin = (member * heads + head) * block_rows
+                part = jnp.where(allowed, scores[begin : begin + block_rows] * scale, MASKED)
+                largest = jnp.max(part, axis=-1, keepdims=True)
+                terms = jnp.exp2(part - largest)
+                masses.append(jnp.sum(terms, axis=-1, keepdims=True))
+                weights.append(terms.astype(jnp.bfloat16))
+        mixed = jnp.dot(
+            jnp.concatenate(weights, axis=0), value_ref[...], preferred_element_type=jnp.float32
+        )
+        for member in range(capacity):
+            index = pack * capacity + member
+            row_base = info_ref[first * capacity + index]
+            limit = info_ref[2 * blocks + first * capacity + index]
+            used = lax.broadcasted_iota(jnp.int32, (block_rows, HEAD_SIZE), 0) + row_base < limit
+            for head in range(heads):
+                begin = (member * heads + head) * block_rows
+                part = mixed[begin : begin + block_rows] / masses[member * heads + head]
+                staged_ref[index, :, head * HEAD_SIZE : (head + 1) * HEAD_SIZE] = jnp.where(
+                    used, part, 0.0
+                ).astype(jnp.bfloat16)
+        rows = pl.ds(pack * capacity, capacity)
+        copy = pltpu.make_async_copy(staged_ref.at[rows], out_ref.at[rows], semaphores.at[pack])
+        copy.start()
+        copies.append(copy)
+    for copy in copies:
+        copy.wait()
+
+
+def attend_part(first, count, capacity, position, info, inverse, place, queries, items):
+    blocks, block_rows, query_cols = queries.shape
+    total = blocks * block_rows
+    pairs = count * block_rows * (query_cols // HEAD_SIZE) * total
+    masks, arrays, offsets = zip(*items)
+    return pl.pallas_call(
+        functools.partial(attend_kernel, first, capacity, masks, offsets),
+        out_shape=jax.ShapeDtypeStruct((count, block_rows, query_cols), jnp.bfloat16),
+        in_specs=[SMEM] * 4 + [VMEM] * (1 + len(items)),
+        out_specs=HBM,
+        scratch_shapes=[
+            pltpu.VMEM((count, block_rows, query_cols), jnp.bfloat16),
+            pltpu.VMEM((total, HEAD_SIZE), jnp.bfloat16),
+            pltpu.VMEM((total, HEAD_SIZE), jnp.bfloat16),
+            pltpu.SemaphoreType.DMA((count // capacity,)),
+        ],
+        compiler_params=ROOM,
+        cost_estimate=pl.CostEstimate(
+            flops=4 * pairs * HEAD_SIZE,
+            bytes_accessed=2 * count * block_rows * (len(items) * 2 * HEAD_SIZE + 2 * query_cols),
+            transcendentals=pairs,
+        ),
+        name="attend_part",
+    )(position, info, inverse, place, queries, *arrays)
+
+
+def project_kernel(first, masks, pieces, inverse_ref, place_ref, weight_ref, *refs):
+    count = len(masks)
+    part_refs = refs[:count]
+    out_ref, gathered_ref, staged_ref, semaphores = refs[-4:]
+    blocks, block_rows, cols = part_refs[0].shape
+    rows = blocks * block_rows
+    place = place_ref[0]
+    features = weight_ref.shape[1]
+    width = features // pieces
+    for mask, part_ref in zip(masks, part_refs):
+        begin = pl.multiple_of(jnp.bitwise_xor(place, mask) * cols, cols)
+        gathered_ref[:, pl.ds(begin, cols)] = part_ref[...].reshape(rows, cols)
+    copies = []
+    for piece in range(pieces):
+        span = slice(piece * width, (piece + 1) * width)
+        total = jnp.dot(
+            gathered_ref[...], weight_ref[:, span], preferred_element_type=jnp.float32
+        )
+        staged_ref[:, :, span] = total.astype(jnp.bfloat16).reshape(blocks, block_rows, width)
+        for index in range(blocks):
+            copy = pltpu.make_async_copy(
+                staged_ref.at[index, :, span],
+                out_ref.at[inverse_ref[first + index], :, span],
+                semaphores.at[piece, index],
+            )
+            copy.start()
+            copies.append(copy)
+    for copy in copies:
+        copy.wait()
+
+
+def project_part(first, inverse, place, out_weight, masks, parts, so_far, out_shape):
+    blocks, block_rows, cols = parts[0].shape
+    features = out_weight.shape[1]
+    operands = [inverse, place, out_weight, *parts]
+    in_specs = [SMEM, SMEM, VMEM] + [VMEM] * len(parts)
+    aliases = {}
+    if so_far is not None:
+        aliases = {len(operands): 0}
+        operands.append(so_far)
+        in_specs.append(HBM)
+    rows = blocks * block_rows
+    pieces = 2
+    return pl.pallas_call(
+        functools.partial(project_kernel, first, masks, pieces),
+        out_shape=jax.ShapeDtypeStruct(out_shape, jnp.bfloat16),
+        in_specs=in_specs,
+        out_specs=HBM,
+        scratch_shapes=[
+            pltpu.VMEM((rows, cols * len(parts)), jnp.bfloat16),
+            pltpu.VMEM((blocks, block_rows, features), jnp.bfloat16),
+            pltpu.SemaphoreType.DMA((pieces, blocks)),
+        ],
+        input_output_aliases=aliases,
+        compiler_params=ROOM,
+        cost_estimate=pl.CostEstimate(
+            flops=2 * rows * cols * len(parts) * features,
+            bytes_accessed=2 * (cols * len(parts) * features + rows * features),
+            transcendentals=0,
+        ),
+        name="project_part",
+    )(*operands)
+
+
+def swap(portion, axis, mask):
+    size = lax.axis_size(axis)
+    return lax.ppermute(portion, axis, [(index, index ^ mask) for index in range(size)])
+
+
+def split_packs(loaders):
+    shares = [share * loaders // sum(SHARES) for share in SHARES]
+    return [(sum(shares[:index]), share) for index, share in enumerate(shares)]
+
+
+def gather_body(queries, keys, values, out_weight, dest_slot, pack_slot, seq_start, seq_len):
+    local_blocks, block_rows, _ = queries.shape
+    loaders = lax.axis_size("dp")
+    shards = lax.axis_size("tensor")
+    capacity = local_blocks // loaders
+    side, near, far = 1, 2, loaders - 2
+    place = lax.axis_index("dp").astype(jnp.int32).reshape(1)
+    shard = lax.axis_index("tensor").astype(jnp.int32).reshape(1)
+    chunks = split_packs(loaders)
+
+    table = jnp.concatenate([pack_slot, seq_start, seq_len], axis=1)
+    inverse, whole, *pieces = sort_blocks(
+        keys, values, dest_slot, [share * capacity for _, share in chunks]
+    )
+    from_far = [swap(piece, "dp", far) for piece in pieces]
+    from_near = swap(whole, "dp", near)
+    from_side = swap(whole, "dp", side)
+    from_both = swap(from_near, "dp", side)
+    order = []
+    for mask in (far, near, side):
+        other = swap(table, "dp", mask)
+        table = jnp.concatenate([table, other], axis=0)
+        order = [m for m in order] + [m ^ mask for m in order] if order else [0, mask]
+    origin = jnp.bitwise_xor(place, jnp.array(order, jnp.int32))
+    tables = jnp.sum(
+        jnp.where(
+            (origin[None, :] == jnp.arange(loaders, dtype=jnp.int32)[:, None])[..., None],
+            table[None],
+            0,
+        ),
+        axis=1,
+    ).reshape(-1)
+    position, info = plan(tables, place, local_blocks, block_rows, capacity)
+    attended = []
+    for index, (first, share) in enumerate(chunks):
+        across = from_far[index]
+        far_near = swap(across, "dp", near)
+        far_side = swap(across, "dp", side)
+        far_both = swap(far_near, "dp", side)
+        begin = first * capacity
+        items = (
+            (0, whole, begin),
+            (side, from_side, begin),
+            (near, from_near, begin),
+            (near ^ side, from_both, begin),
+            (far, across, 0),
+            (far ^ side, far_side, 0),
+            (far ^ near, far_near, 0),
+            (far ^ near ^ side, far_both, 0),
+        )
+        attended.append(
+            attend_part(
+                first, share * capacity, capacity, position, info, inverse, place, queries, items
+            )
+        )
+    result = None
+    out_shape = (local_blocks, block_rows, out_weight.shape[1])
+    for (first, share), part in zip(chunks, attended):
+        partner = swap(part, "tensor", 1)
+        opposite = swap(part, "tensor", shards // 2)
+        both = swap(opposite, "tensor", 1)
+        result = project_part(
+            first * capacity,
+            inverse,
+            shard,
+            out_weight,
+            (0, 1, shards // 2, shards // 2 + 1),
+            (part, partner, opposite, both),
+            result,
+            out_shape,
+        )
+    return result
 
 
 def solution(mesh):
@@ -125,6 +452,13 @@
         P("dp", None),
         P("dp", None),
     )
+    gathers = mesh.shape["dp"] == 2**3 and mesh.shape["tensor"] == 2**2
+
+    def body(*args):
+        if not gathers:
+            return exchange_body(*args)
+        return gather_body(*args)
+
     return jax.shard_map(
         body, mesh=mesh, in_specs=placed, out_specs=P("dp", None, "tensor"), check_vma=False
     )

time: 169 us -> 113 us (0.67)
  waiting for transfers between devices: 87.4 us -> 32.7 us
  Pallas kernels: 0 us -> 32.5 us
  local copies, waits for them, and re-layouts: 24.6 us -> 9.23 us
  starting transfers between devices: 18.6 us -> 33.7 us
  matrix products: 14 us -> 0 us
  between operations: 13.7 us -> 0.36 us
  other arithmetic: 9.95 us -> 3.81 us
    all_to_all x4 -> x0, waiting for transfers between devices: 53.7 us -> none  [the longest x1 25.5 us: body(): lax.all_to_all(going_back, 'dp', split_axis=0, concat_axis=0, tiled=True)]
    all_gather x1 -> x0, waiting for transfers between devices: 33.7 us -> none  [body(): lax.all_gather(own_rows, 'tensor', axis=1, tiled=True)]
    ppermute x0 -> x27, starting transfers between devices: none -> 33.7 us  [swap(): lax.ppermute(portion, axis, [(index, index ^ mask) for index in range(siz...]
    ppermute x0 -> x27, waiting for transfers between devices: none -> 32.7 us  [swap(): lax.ppermute(portion, axis, [(index, index ^ mask) for index in range(siz...]
    pallas_call x0 -> x8, Pallas kernels: none -> 32.5 us  [the longest x3 17.4 us: attend_part(): pl.pallas_call(functools.partial(attend_kernel, first, capacity, masks, o...]
    all_to_all x4 -> x0, starting transfers between devices: 18.4 us -> none  [the longest x1 7.28 us: body(): lax.all_to_all(outgoing(values), 'dp', split_axis=0, concat_axis=0, tiled...]
    scatter x4 -> x0, local copies, waits for them, and re-layouts: 17.7 us -> none  [the longest x3 13.1 us: outgoing(): jnp.zeros((slot_count,) + portion.shape[1:], portion.dtype).at[dest_slot]]
    dot_general x7 -> x0, matrix products: 14 us -> none  [the longest x1 9.27 us: body(): jnp.dot(lax.all_gather(own_rows, 'tensor', axis=1, tiled=True), out_weigh...]
  transfers between devices with their start and end apart: 5 -> 27, of which waited for: 5 -> 8; matrix products, arithmetic and copies ran while one was open for 9% -> 3% of each run, Pallas kernels for 0% -> 25%
where the time goes in v1:
time: 113 us; the launch traced here: 112 us
  starting transfers between devices  33.7 us (30%)
  waiting for transfers between devices  32.7 us (29%)
  Pallas kernels  32.5 us (29%)
  local copies, waits for them, and re-layouts  9.23 us (8%)
  other arithmetic  3.81 us (3%)
    ppermute x27, starting transfers between devices, swap(): lax.ppermute(portion, axis, [(index, index ^ mask) for index in range(siz...  33.7 us
    ppermute x27, waiting for transfers between devices, swap(): lax.ppermute(portion, axis, [(index, index ^ mask) for index in range(siz...  32.7 us
    pallas_call x3, Pallas kernels, attend_part(): pl.pallas_call(functools.partial(attend_kernel, first, capacity, masks, o...  17.4 us
    pallas_call x3, Pallas kernels, project_part(): pl.pallas_call(functools.partial(project_kernel, first, masks, pieces), o...  10.7 us
    unnamed x24, local copies, waits for them, and re-layouts  9.15 us
    pallas_call x1, Pallas kernels, plan(): pl.pallas_call(functools.partial(plan_kernel, block_rows, capacity), out_...  3.12 us
    concatenate x3, other arithmetic, gather_body(): table = jnp.concatenate([table, other], axis=0)  2.29 us
  transfers between devices with their start and end apart: 27, of which 8 were waited for; matrix products, arithmetic and copies ran while one was open for 3% of the time, Pallas kernels for 25%

profile of v1, /device:TPU:0, one launch (start us, length us, event | category | flops | bytes accessed | tf_op | source)
XLA Modules:
  0.0 112.2 jit_solution(11364412990147373033)
XLA Ops:
  0.0 0.9 copy-done.3
  1.0 0.9 copy-done.4
  1.9 0.7 copy-done.9
  2.6 1.3 %sort_blocks.1 = (s32[32]{0:T(128)S(1)}, bf16[32,32,256]{2,1,0:T(8,128)(2,1)S(1)}, bf16[12,32,256]{2,1,0:T(8,128)(2,1)S(1)}, bf16[12,32,256]{2,1,0:T(8,128)(2,1)S(1)}, bf16[8,32,256]{2,1,0:T(8,128)(2,1)S(1)}) custom-call(s32[32]{0:T(128)S(1)} %copy-done.9, bf16[32,32,128]{2,1,0:T(8,128)(2,1)S(1)} %copy-done.3, bf16[32,32,128]{2,1,0:T(8,128)(2,1)S(1)} %copy-done.4), custom_call_target="tpu_custom_call" | custom-call | tf_op jit(solution)/shard_map/sort_blocks/pallas_call | solution.py:138
  3.9 0.6 copy-done.10
  4.5 3.1 %collective-permute-start.4 = (bf16[32,32,256]{2,1,0:T(8,128)(2,1)S(1)}, bf16[32,32,256]{2,1,0:T(8,128)(2,1)S(1)}, u32[]{:S(2)}, u32[]{:S(2)}) collective-permute-start(bf16[32,32,256]{2,1,0:T(8,128)(2,1)S(1)} %get-tuple-element.15.refs_0_), channel_id=1, source_target_pairs={{0,8},{4,12},{8,0},{12,4},{16,24},{20,28},{24,16},{28,20},{1,9},{5... | collective-permute-start | bytes 1572872 | tf_op jit(solution)/shard_map/ppermute | solution.py:362
  7.6 0.8 pad_add_fusion.3
  8.3 2.5 %collective-permute-start = (s32[1,96]{1,0:T(1,128)S(1)}, s32[1,96]{1,0:T(1,128)S(1)}, u32[]{:S(2)}, u32[]{:S(2)}) collective-permute-start(s32[1,96]{1,0:T(1,128)S(1)} %pad_add_fusion.3), channel_id=1, source_target_pairs={{0,24},{4,28},{8,16},{12,20},{16,8},{20,12},{24,0},{28,4},{1,25},{... | collective-permute-start | bytes 1160 | tf_op jit(solution)/shard_map/ppermute | solution.py:362
  10.8 10.9 %collective-permute-done = s32[1,96]{1,0:T(1,128)S(1)} collective-permute-done((s32[1,96]{1,0:T(1,128)S(1)}, s32[1,96]{1,0:T(1,128)S(1)}, u32[]{:S(2)}, u32[]{:S(2)}) %collective-permute-start) | collective-permute-done | bytes 416 | tf_op jit(solution)/shard_map/ppermute | solution.py:362
  21.7 0.8 pad_add_fusion.2
  22.5 1.6 %collective-permute-start.3 = (bf16[32,32,256]{2,1,0:T(8,128)(2,1)S(1)}, bf16[32,32,256]{2,1,0:T(8,128)(2,1)S(1)}, u32[]{:S(2)}, u32[]{:S(2)}) collective-permute-start(bf16[32,32,256]{2,1,0:T(8,128)(2,1)S(1)} %get-tuple-element.15.refs_0_), channel_id=1, source_target_pairs={{0,4},{4,0},{8,12},{12,8},{16,20},{20,16},{24,28},{28,24},{1,5},{5... | collective-permute-start | bytes 1572872 | tf_op jit(solution)/shard_map/ppermute | solution.py:362
  24.0 1.4 %collective-permute-start.13 = (bf16[12,32,256]{2,1,0:T(8,128)(2,1)S(1)}, bf16[12,32,256]{2,1,0:T(8,128)(2,1)S(1)}, u32[]{:S(2)}, u32[]{:S(2)}) collective-permute-start(bf16[12,32,256]{2,1,0:T(8,128)(2,1)S(1)} %get-tuple-element.17), channel_id=1, source_target_pairs={{0,24},{4,28},{8,16},{12,20},{16,8},{20,12},{24,0},{28,4},{1,25},{... | collective-permute-start | bytes 589832 | tf_op jit(solution)/shard_map/ppermute | solution.py:362
  25.4 2.5 %collective-permute-start.20 = (bf16[12,32,256]{2,1,0:T(8,128)(2,1)S(1)}, bf16[12,32,256]{2,1,0:T(8,128)(2,1)S(1)}, u32[]{:S(2)}, u32[]{:S(2)}) collective-permute-start(bf16[12,32,256]{2,1,0:T(8,128)(2,1)S(1)} %get-tuple-element.18), channel_id=1, source_target_pairs={{0,24},{4,28},{8,16},{12,20},{16,8},{20,12},{24,0},{28,4},{1,25},{... | collective-permute-start | bytes 589832 | tf_op jit(solution)/shard_map/ppermute | solution.py:362
  27.9 0.8 pad_add_fusion.1
  28.6 0.5 collective-permute-start.2
  29.2 1.5 %collective-permute-start.5 = (bf16[32,32,256]{2,1,0:T(8,128)(2,1)S(1)}, bf16[32,32,256]{2,1,0:T(8,128)(2,1)S(1)}, u32[]{:S(2)}, u32[]{:S(2)}) collective-permute-start(bf16[32,32,256]{2,1,0:T(8,128)(2,1)S(1)} %collective-permute-done.4.refs_2_), channel_id=1, source_target_pairs={{0,4},{4,0},{8,12},{12,8},{16,20},{20,16},{24,28},{28,24},{1,5},{5... | collective-permute-start | bytes 1572872 | tf_op jit(solution)/shard_map/ppermute | solution.py:362
  30.7 0.7 broadcast_xor_fusion
  31.3 4.0 %collective-permute-done.20.refs_4_ = bf16[12,32,256]{2,1,0:T(8,128)(2,1)S(1)} collective-permute-done((bf16[12,32,256]{2,1,0:T(8,128)(2,1)S(1)}, bf16[12,32,256]{2,1,0:T(8,128)(2,1)S(1)}, u32[]{:S(2)}, u32[]{:S(2)}) %collective-permute-start.20) | collective-permute-done | bytes 196640 | tf_op jit(solution)/shard_map/ppermute | solution.py:362
  35.4 8.2 %collective-permute-start.22 = (bf16[12,32,256]{2,1,0:T(8,128)(2,1)S(1)}, bf16[12,32,256]{2,1,0:T(8,128)(2,1)S(1)}, u32[]{:S(2)}, u32[]{:S(2)}) collective-permute-start(bf16[12,32,256]{2,1,0:T(8,128)(2,1)S(1)} %collective-permute-done.20.refs_4_), channel_id=1, source_target_pairs={{0,8},{4,12},{8,0},{12,4},{16,24},{20,28},{24,16},{28,20},{1,9},{5... | collective-permute-start | bytes 589832 | tf_op jit(solution)/shard_map/ppermute | solution.py:362
  43.6 0.5 collective-permute-start.21
  44.1 5.2 %collective-permute-done.22.refs_6_ = bf16[12,32,256]{2,1,0:T(8,128)(2,1)S(1)} collective-permute-done((bf16[12,32,256]{2,1,0:T(8,128)(2,1)S(1)}, bf16[12,32,256]{2,1,0:T(8,128)(2,1)S(1)}, u32[]{:S(2)}, u32[]{:S(2)}) %collective-permute-start.22) | collective-permute-done | bytes 196640 | tf_op jit(solution)/shard_map/ppermute | solution.py:362
  49.3 0.5 collective-permute-start.23
  49.8 0.8 pad_add_fusion
  50.6 1.5 %collective-permute-done.15.refs_6_ = bf16[12,32,256]{2,1,0:T(8,128)(2,1)S(1)} collective-permute-done((bf16[12,32,256]{2,1,0:T(8,128)(2,1)S(1)}, bf16[12,32,256]{2,1,0:T(8,128)(2,1)S(1)}, u32[]{:S(2)}, u32[]{:S(2)}) %collective-permute-start.15) | collective-permute-done | bytes 196640 | tf_op jit(solution)/shard_map/ppermute | solution.py:362
  52.2 0.5 collective-permute-start.14
  52.7 1.5 %collective-permute-start.16 = (bf16[12,32,256]{2,1,0:T(8,128)(2,1)S(1)}, bf16[12,32,256]{2,1,0:T(8,128)(2,1)}, u32[]{:S(2)}, u32[]{:S(2)}) collective-permute-start(bf16[12,32,256]{2,1,0:T(8,128)(2,1)S(1)} %collective-permute-done.15.refs_6_), channel_id=1, source_target_pairs={{0,4},{4,0},{8,12},{12,8},{16,20},{20,16},{24,28},{28,24},{1,5},{5... | collective-permute-start | bytes 589832 | tf_op jit(solution)/shard_map/ppermute | solution.py:362
  54.3 3.1 %plan.1 = (s32[256]{0:T(256)S(1)}, s32[96]{0:T(128)S(1)}) custom-call(s32[768]{0:T(1024)S(1)} %reshape.30.tables_ref, s32[1]{0:T(128)} %bitcast.1.place_ref), custom_call_target="tpu_custom_call" | custom-call | tf_op jit(solution)/shard_map/plan/pallas_call | solution.py:184
  57.5 0.7 copy-done.7
  58.2 1.2 %copy-done.2 = bf16[32,32,512]{2,1,0:T(8,128)(2,1)S(1)} copy-done((bf16[32,32,512]{2,1,0:T(8,128)(2,1)S(1)}, bf16[32,32,512]{2,1,0:T(8,128)(2,1)}, u32[]{:S(2)}) %copy-start.2) | copy-done | bytes 1048600
  59.4 0.9 copy-done.8
  60.3 6.2 %attend_part.5.refs_0_ = bf16[12,32,512]{2,1,0:T(8,128)(2,1)S(1)} custom-call(s32[256]{0:T(256)S(1)} %get-tuple-element.13.position_ref, s32[96]{0:T(128)S(1)} %get-tuple-element.14.info_ref, s32[32]{0:T(128)S(1)} %get-tuple-element.12.inverse_ref, s32[1]{0:T(128)} %bitcast.1.place_ref, bf16[32,32,512]{2,1,0:T(8,128)(2,1)S(1)} %copy-done.2, ...), custom_call_target="tpu_custom_call" | custom-call | flops 805306368 | bytes 2359296 | tf_op jit(solution)/shard_map/attend_part/pallas_call | solution.py:275
  66.5 1.6 %collective-permute-start.25 = (bf16[12,32,512]{2,1,0:T(8,128)(2,1)S(1)}, bf16[12,32,512]{2,1,0:T(8,128)(2,1)S(1)}, u32[]{:S(2)}, u32[]{:S(2)}) collective-permute-start(bf16[12,32,512]{2,1,0:T(8,128)(2,1)S(1)} %attend_part.5.refs_0_), channel_id=1, source_target_pairs={{0,2},{1,3},{2,0},{3,1},{4,6},{5,7},{6,4},{7,5},{8,10},{9,11},{10,... | collective-permute-start | bytes 1179656 | tf_op jit(solution)/shard_map/ppermute | solution.py:362
  68.1 1.4 %collective-permute-start.6 = (bf16[8,32,256]{2,1,0:T(8,128)(2,1)S(1)}, bf16[8,32,256]{2,1,0:T(8,128)(2,1)S(1)}, u32[]{:S(2)}, u32[]{:S(2)}) collective-permute-start(bf16[8,32,256]{2,1,0:T(8,128)(2,1)S(1)} %copy-done.11), channel_id=1, source_target_pairs={{0,24},{4,28},{8,16},{12,20},{16,8},{20,12},{24,0},{28,4},{1,25},{... | collective-permute-start | bytes 393224 | tf_op jit(solution)/shard_map/ppermute | solution.py:362
  69.5 0.9 copy-done.6
  70.4 6.9 %attend_part.4.refs_0_ = bf16[12,32,512]{2,1,0:T(8,128)(2,1)S(1)} custom-call(s32[256]{0:T(256)S(1)} %get-tuple-element.13.position_ref, s32[96]{0:T(128)S(1)} %get-tuple-element.14.info_ref, s32[32]{0:T(128)S(1)} %get-tuple-element.12.inverse_ref, s32[1]{0:T(128)} %bitcast.1.place_ref, bf16[32,32,512]{2,1,0:T(8,128)(2,1)S(1)} %copy-done.2, ...), custom_call_target="tpu_custom_call" | custom-call | flops 805306368 | bytes 2359296 | tf_op jit(solution)/shard_map/attend_part/pallas_call | solution.py:275
  77.3 0.6 collective-permute-start.18
  77.9 1.1 collective-permute-start.8
  78.9 0.9 collective-permute-start.7
  79.8 3.0 %collective-permute-done.8.refs_6_ = bf16[8,32,256]{2,1,0:T(8,128)(2,1)S(1)} collective-permute-done((bf16[8,32,256]{2,1,0:T(8,128)(2,1)S(1)}, bf16[8,32,256]{2,1,0:T(8,128)(2,1)S(1)}, u32[]{:S(2)}, u32[]{:S(2)}) %collective-permute-start.8) | collective-permute-done | bytes 131104 | tf_op jit(solution)/shard_map/ppermute | solution.py:362
  82.8 0.9 collective-permute-start.9
  84.4 3.4 %collective-permute-done.9.refs_7_ = bf16[8,32,256]{2,1,0:T(8,128)(2,1)S(1)} collective-permute-done((bf16[8,32,256]{2,1,0:T(8,128)(2,1)S(1)}, bf16[8,32,256]{2,1,0:T(8,128)(2,1)S(1)}, u32[]{:S(2)}, u32[]{:S(2)}) %collective-permute-start.9) | collective-permute-done | bytes 131104 | tf_op jit(solution)/shard_map/ppermute | solution.py:362
  87.8 4.3 %attend_part.3.refs_0_ = bf16[8,32,512]{2,1,0:T(8,128)(2,1)S(1)} custom-call(s32[256]{0:T(256)S(1)} %get-tuple-element.13.position_ref, s32[96]{0:T(128)S(1)} %get-tuple-element.14.info_ref, s32[32]{0:T(128)S(1)} %get-tuple-element.12.inverse_ref, s32[1]{0:T(128)} %bitcast.1.place_ref, bf16[32,32,512]{2,1,0:T(8,128)(2,1)S(1)} %copy-done.2, ...), custom_call_target="tpu_custom_call" | custom-call | flops 536870912 | bytes 1572864 | tf_op jit(solution)/shard_map/attend_part/pallas_call | solution.py:275
  92.1 1.6 %collective-permute-start.11 = (bf16[8,32,512]{2,1,0:T(8,128)(2,1)S(1)}, bf16[8,32,512]{2,1,0:T(8,128)(2,1)S(1)}, u32[]{:S(2)}, u32[]{:S(2)}) collective-permute-start(bf16[8,32,512]{2,1,0:T(8,128)(2,1)S(1)} %attend_part.3.refs_0_), channel_id=1, source_target_pairs={{0,2},{1,3},{2,0},{3,1},{4,6},{5,7},{6,4},{7,5},{8,10},{9,11},{10,... | collective-permute-start | bytes 786440 | tf_op jit(solution)/shard_map/ppermute | solution.py:362
  94.2 4.3 %collective-permute-done.11.refs_2_ = bf16[8,32,512]{2,1,0:T(8,128)(2,1)S(1)} collective-permute-done((bf16[8,32,512]{2,1,0:T(8,128)(2,1)S(1)}, bf16[8,32,512]{2,1,0:T(8,128)(2,1)S(1)}, u32[]{:S(2)}, u32[]{:S(2)}) %collective-permute-start.11) | collective-permute-done | bytes 262176 | tf_op jit(solution)/shard_map/ppermute | solution.py:362
  99.1 2.2 %copy-done = bf16[2048,1024]{1,0:T(8,128)(2,1)S(1)} copy-done((bf16[2048,1024]{1,0:T(8,128)(2,1)S(1)}, bf16[2048,1024]{1,0:T(8,128)(2,1)}, u32[]{:S(2)}) %copy-start) | copy-done | bytes 4194328
  101.3 4.0 %project_part.3.refs_4_ = bf16[32,32,1024]{2,1,0:T(8,128)(2,1)} custom-call(s32[32]{0:T(128)S(1)} %get-tuple-element.12.inverse_ref, s32[1]{0:T(128)} %bitcast.place_ref, bf16[2048,1024]{1,0:T(8,128)(2,1)S(1)} %copy-done, bf16[12,32,512]{2,1,0:T(8,128)(2,1)S(1)} %attend_part.5.refs_0_, bf16[12,32,512]{2,1,0:T(8,128)(2,1)} %collective-permute-done.24.refs_1_, ...), custom_call_target="tpu_custom_call" | custom-call | flops 1610612736 | bytes 4980736 | tf_op jit(solution)/shard_map/project_part/pallas_call | solution.py:339
  105.3 4.0 %project_part.4.refs_4_ = bf16[32,32,1024]{2,1,0:T(8,128)(2,1)} custom-call(s32[32]{0:T(128)S(1)} %get-tuple-element.12.inverse_ref, s32[1]{0:T(128)} %bitcast.place_ref, bf16[2048,1024]{1,0:T(8,128)(2,1)S(1)} %copy-done, bf16[12,32,512]{2,1,0:T(8,128)(2,1)S(1)} %attend_part.4.refs_0_, ...), custom_call_target="tpu_custom_call", output_to_operand_aliasing={{}: (7, {})} | custom-call | flops 1610612736 | bytes 4980736 | tf_op jit(solution)/shard_map/project_part/pallas_call | solution.py:339
  109.3 2.7 %project_part.5 = bf16[32,32,1024]{2,1,0:T(8,128)(2,1)} custom-call(s32[32]{0:T(128)S(1)} %get-tuple-element.12.inverse_ref, s32[1]{0:T(128)} %bitcast.place_ref, bf16[2048,1024]{1,0:T(8,128)(2,1)S(1)} %copy-done.1, bf16[8,32,512]{2,1,0:T(8,128)(2,1)S(1)} %attend_part.3.refs_0_, ...), custom_call_target="tpu_custom_call", output_to_operand_aliasing={{}: (7, {})} | custom-call | flops 1073741824 | bytes 4718592 | tf_op jit(solution)/shard_map/project_part/pallas_call | solution.py:339
  (46 shorter events, 2.0 us)
Async XLA Ops:
  0.0 0.9 copy-start.3
  1.0 0.9 copy-start.4
  1.9 0.7 copy-start.9
  3.9 0.7 copy-start.10
  4.5 24.6 %collective-permute-start.4 = (bf16[32,32,256]{2,1,0:T(8,128)(2,1)S(1)}, bf16[32,32,256]{2,1,0:T(8,128)(2,1)S(1)}, u32[]{:S(2)}, u32[]{:S(2)}) collective-permute-start(bf16[32,32,256]{2,1,0:T(8,128)(2,1)S(1)} %get-tuple-element.15.refs_0_), channel_id=1, source_target_pairs={{0,8},{4,12},{8,0},{12,4},{16,24},{20,28},{24,16},{28,20},{1,9},{5... | collective-permute-start | bytes 1572872 | tf_op jit(solution)/shard_map/ppermute | solution.py:362
  8.3 13.4 %collective-permute-start = (s32[1,96]{1,0:T(1,128)S(1)}, s32[1,96]{1,0:T(1,128)S(1)}, u32[]{:S(2)}, u32[]{:S(2)}) collective-permute-start(s32[1,96]{1,0:T(1,128)S(1)} %pad_add_fusion.3), channel_id=1, source_target_pairs={{0,24},{4,28},{8,16},{12,20},{16,8},{20,12},{24,0},{28,4},{1,25},{... | collective-permute-start | bytes 1160 | tf_op jit(solution)/shard_map/ppermute | solution.py:362
  22.5 5.4 %collective-permute-start.1 = (s32[2,96]{1,0:T(2,128)S(1)}, s32[2,96]{1,0:T(2,128)S(1)}, u32[]{:S(2)}, u32[]{:S(2)}) collective-permute-start(s32[2,96]{1,0:T(2,128)S(1)} %pad_add_fusion.2), channel_id=1, source_target_pairs={{0,8},{4,12},{8,0},{12,4},{16,24},{20,28},{24,16},{28,20},{1,9},{5... | collective-permute-start | bytes 2312 | tf_op jit(solution)/shard_map/ppermute | solution.py:362
  22.5 35.0 %collective-permute-start.3 = (bf16[32,32,256]{2,1,0:T(8,128)(2,1)S(1)}, bf16[32,32,256]{2,1,0:T(8,128)(2,1)S(1)}, u32[]{:S(2)}, u32[]{:S(2)}) collective-permute-start(bf16[32,32,256]{2,1,0:T(8,128)(2,1)S(1)} %get-tuple-element.15.refs_0_), channel_id=1, source_target_pairs={{0,4},{4,0},{8,12},{12,8},{16,20},{20,16},{24,28},{28,24},{1,5},{5... | collective-permute-start | bytes 1572872 | tf_op jit(solution)/shard_map/ppermute | solution.py:362
  24.0 20.1 %collective-permute-start.13 = (bf16[12,32,256]{2,1,0:T(8,128)(2,1)S(1)}, bf16[12,32,256]{2,1,0:T(8,128)(2,1)S(1)}, u32[]{:S(2)}, u32[]{:S(2)}) collective-permute-start(bf16[12,32,256]{2,1,0:T(8,128)(2,1)S(1)} %get-tuple-element.17), channel_id=1, source_target_pairs={{0,24},{4,28},{8,16},{12,20},{16,8},{20,12},{24,0},{28,4},{1,25},{... | collective-permute-start | bytes 589832 | tf_op jit(solution)/shard_map/ppermute | solution.py:362
  25.4 10.0 %collective-permute-start.20 = (bf16[12,32,256]{2,1,0:T(8,128)(2,1)S(1)}, bf16[12,32,256]{2,1,0:T(8,128)(2,1)S(1)}, u32[]{:S(2)}, u32[]{:S(2)}) collective-permute-start(bf16[12,32,256]{2,1,0:T(8,128)(2,1)S(1)} %get-tuple-element.18), channel_id=1, source_target_pairs={{0,24},{4,28},{8,16},{12,20},{16,8},{20,12},{24,0},{28,4},{1,25},{... | collective-permute-start | bytes 589832 | tf_op jit(solution)/shard_map/ppermute | solution.py:362
  28.6 14.9 %collective-permute-start.2 = (s32[4,96]{1,0:T(4,128)S(1)}, s32[4,96]{1,0:T(4,128)S(1)}, u32[]{:S(2)}, u32[]{:S(2)}) collective-permute-start(s32[4,96]{1,0:T(4,128)S(1)} %pad_add_fusion.1), channel_id=1, source_target_pairs={{0,4},{4,0},{8,12},{12,8},{16,20},{20,16},{24,28},{28,24},{1,5},{5... | collective-permute-start | bytes 4616 | tf_op jit(solution)/shard_map/ppermute | solution.py:362
  29.2 29.0 %collective-permute-start.5 = (bf16[32,32,256]{2,1,0:T(8,128)(2,1)S(1)}, bf16[32,32,256]{2,1,0:T(8,128)(2,1)S(1)}, u32[]{:S(2)}, u32[]{:S(2)}) collective-permute-start(bf16[32,32,256]{2,1,0:T(8,128)(2,1)S(1)} %collective-permute-done.4.refs_2_), channel_id=1, source_target_pairs={{0,4},{4,0},{8,12},{12,8},{16,20},{20,16},{24,28},{28,24},{1,5},{5... | collective-permute-start | bytes 1572872 | tf_op jit(solution)/shard_map/ppermute | solution.py:362
  35.4 13.9 %collective-permute-start.22 = (bf16[12,32,256]{2,1,0:T(8,128)(2,1)S(1)}, bf16[12,32,256]{2,1,0:T(8,128)(2,1)S(1)}, u32[]{:S(2)}, u32[]{:S(2)}) collective-permute-start(bf16[12,32,256]{2,1,0:T(8,128)(2,1)S(1)} %collective-permute-done.20.refs_4_), channel_id=1, source_target_pairs={{0,8},{4,12},{8,0},{12,4},{16,24},{20,28},{24,16},{28,20},{1,9},{5... | collective-permute-start | bytes 589832 | tf_op jit(solution)/shard_map/ppermute | solution.py:362
  43.6 9.1 %collective-permute-start.21 = (bf16[12,32,256]{2,1,0:T(8,128)(2,1)S(1)}, bf16[12,32,256]{2,1,0:T(8,128)(2,1)S(1)}, u32[]{:S(2)}, u32[]{:S(2)}) collective-permute-start(bf16[12,32,256]{2,1,0:T(8,128)(2,1)S(1)} %collective-permute-done.20.refs_4_), channel_id=1, source_target_pairs={{0,4},{4,0},{8,12},{12,8},{16,20},{20,16},{24,28},{28,24},{1,5},{5... | collective-permute-start | bytes 589832 | tf_op jit(solution)/shard_map/ppermute | solution.py:362
  44.1 8.1 %collective-permute-start.15 = (bf16[12,32,256]{2,1,0:T(8,128)(2,1)S(1)}, bf16[12,32,256]{2,1,0:T(8,128)(2,1)S(1)}, u32[]{:S(2)}, u32[]{:S(2)}) collective-permute-start(bf16[12,32,256]{2,1,0:T(8,128)(2,1)S(1)} %collective-permute-done.13.refs_4_), channel_id=1, source_target_pairs={{0,8},{4,12},{8,0},{12,4},{16,24},{20,28},{24,16},{28,20},{1,9},{5... | collective-permute-start | bytes 589832 | tf_op jit(solution)/shard_map/ppermute | solution.py:362
  49.3 8.2 %collective-permute-start.23 = (bf16[12,32,256]{2,1,0:T(8,128)(2,1)S(1)}, bf16[12,32,256]{2,1,0:T(8,128)(2,1)S(1)}, u32[]{:S(2)}, u32[]{:S(2)}) collective-permute-start(bf16[12,32,256]{2,1,0:T(8,128)(2,1)S(1)} %collective-permute-done.22.refs_6_), channel_id=1, source_target_pairs={{0,4},{4,0},{8,12},{12,8},{16,20},{20,16},{24,28},{28,24},{1,5},{5... | collective-permute-start | bytes 589832 | tf_op jit(solution)/shard_map/ppermute | solution.py:362
  52.1 14.4 %copy-start.5 = (bf16[12,32,256]{2,1,0:T(8,128)(2,1)}, bf16[12,32,256]{2,1,0:T(8,128)(2,1)S(1)}, u32[]{:S(2)}) copy-start(bf16[12,32,256]{2,1,0:T(8,128)(2,1)S(1)} %collective-permute-done.15.refs_6_) | copy-start | bytes 589828
  52.2 17.3 %collective-permute-start.14 = (bf16[12,32,256]{2,1,0:T(8,128)(2,1)S(1)}, bf16[12,32,256]{2,1,0:T(8,128)(2,1)}, u32[]{:S(2)}, u32[]{:S(2)}) collective-permute-start(bf16[12,32,256]{2,1,0:T(8,128)(2,1)S(1)} %collective-permute-done.13.refs_4_), channel_id=1, source_target_pairs={{0,4},{4,0},{8,12},{12,8},{16,20},{20,16},{24,28},{28,24},{1,5},{5... | collective-permute-start | bytes 589832 | tf_op jit(solution)/shard_map/ppermute | solution.py:362
  52.7 16.8 %collective-permute-start.16 = (bf16[12,32,256]{2,1,0:T(8,128)(2,1)S(1)}, bf16[12,32,256]{2,1,0:T(8,128)(2,1)}, u32[]{:S(2)}, u32[]{:S(2)}) collective-permute-start(bf16[12,32,256]{2,1,0:T(8,128)(2,1)S(1)} %collective-permute-done.15.refs_6_), channel_id=1, source_target_pairs={{0,4},{4,0},{8,12},{12,8},{16,20},{20,16},{24,28},{28,24},{1,5},{5... | collective-permute-start | bytes 589832 | tf_op jit(solution)/shard_map/ppermute | solution.py:362
  57.5 0.7 copy-start.7
  58.2 1.2 %copy-start.2 = (bf16[32,32,512]{2,1,0:T(8,128)(2,1)S(1)}, bf16[32,32,512]{2,1,0:T(8,128)(2,1)}, u32[]{:S(2)}) copy-start(bf16[32,32,512]{2,1,0:T(8,128)(2,1)} %query_ref.5) | copy-start | bytes 3145732
  59.4 0.9 copy-start.8
  60.3 7.8 %copy-start.11 = (bf16[8,32,256]{2,1,0:T(8,128)(2,1)S(1)}, bf16[8,32,256]{2,1,0:T(8,128)(2,1)}, u32[]{:S(2)}) copy-start(bf16[8,32,256]{2,1,0:T(8,128)(2,1)} %copy-done.10) | copy-start | bytes 393220
  66.5 17.1 %collective-permute-start.25 = (bf16[12,32,512]{2,1,0:T(8,128)(2,1)S(1)}, bf16[12,32,512]{2,1,0:T(8,128)(2,1)S(1)}, u32[]{:S(2)}, u32[]{:S(2)}) collective-permute-start(bf16[12,32,512]{2,1,0:T(8,128)(2,1)S(1)} %attend_part.5.refs_0_), channel_id=1, source_target_pairs={{0,2},{1,3},{2,0},{3,1},{4,6},{5,7},{6,4},{7,5},{8,10},{9,11},{10,... | collective-permute-start | bytes 1179656 | tf_op jit(solution)/shard_map/ppermute | solution.py:362
  68.1 9.7 %collective-permute-start.6 = (bf16[8,32,256]{2,1,0:T(8,128)(2,1)S(1)}, bf16[8,32,256]{2,1,0:T(8,128)(2,1)S(1)}, u32[]{:S(2)}, u32[]{:S(2)}) collective-permute-start(bf16[8,32,256]{2,1,0:T(8,128)(2,1)S(1)} %copy-done.11), channel_id=1, source_target_pairs={{0,24},{4,28},{8,16},{12,20},{16,8},{20,12},{24,0},{28,4},{1,25},{... | collective-permute-start | bytes 393224 | tf_op jit(solution)/shard_map/ppermute | solution.py:362
  69.5 0.9 copy-start.6
  77.3 16.4 %collective-permute-start.18 = (bf16[12,32,512]{2,1,0:T(8,128)(2,1)S(1)}, bf16[12,32,512]{2,1,0:T(8,128)(2,1)}, u32[]{:S(2)}, u32[]{:S(2)}) collective-permute-start(bf16[12,32,512]{2,1,0:T(8,128)(2,1)S(1)} %attend_part.4.refs_0_), channel_id=1, source_target_pairs={{0,2},{1,3},{2,0},{3,1},{4,6},{5,7},{6,4},{7,5},{8,10},{9,11},{10,... | collective-permute-start | bytes 1179656 | tf_op jit(solution)/shard_map/ppermute | solution.py:362
  77.9 5.0 %collective-permute-start.8 = (bf16[8,32,256]{2,1,0:T(8,128)(2,1)S(1)}, bf16[8,32,256]{2,1,0:T(8,128)(2,1)S(1)}, u32[]{:S(2)}, u32[]{:S(2)}) collective-permute-start(bf16[8,32,256]{2,1,0:T(8,128)(2,1)S(1)} %collective-permute-done.6.refs_4_), channel_id=1, source_target_pairs={{0,8},{4,12},{8,0},{12,4},{16,24},{20,28},{24,16},{28,20},{1,9},{5... | collective-permute-start | bytes 393224 | tf_op jit(solution)/shard_map/ppermute | solution.py:362
  78.9 5.5 %collective-permute-start.7 = (bf16[8,32,256]{2,1,0:T(8,128)(2,1)S(1)}, bf16[8,32,256]{2,1,0:T(8,128)(2,1)S(1)}, u32[]{:S(2)}, u32[]{:S(2)}) collective-permute-start(bf16[8,32,256]{2,1,0:T(8,128)(2,1)S(1)} %collective-permute-done.6.refs_4_), channel_id=1, source_target_pairs={{0,4},{4,0},{8,12},{12,8},{16,20},{20,16},{24,28},{28,24},{1,5},{5... | collective-permute-start | bytes 393224 | tf_op jit(solution)/shard_map/ppermute | solution.py:362
  82.8 5.0 %collective-permute-start.9 = (bf16[8,32,256]{2,1,0:T(8,128)(2,1)S(1)}, bf16[8,32,256]{2,1,0:T(8,128)(2,1)S(1)}, u32[]{:S(2)}, u32[]{:S(2)}) collective-permute-start(bf16[8,32,256]{2,1,0:T(8,128)(2,1)S(1)} %collective-permute-done.8.refs_6_), channel_id=1, source_target_pairs={{0,4},{4,0},{8,12},{12,8},{16,20},{20,16},{24,28},{28,24},{1,5},{5... | collective-permute-start | bytes 393224 | tf_op jit(solution)/shard_map/ppermute | solution.py:362
  83.7 14.9 %collective-permute-start.24 = (bf16[12,32,512]{2,1,0:T(8,128)(2,1)S(1)}, bf16[12,32,512]{2,1,0:T(8,128)(2,1)}, u32[]{:S(2)}, u32[]{:S(2)}) collective-permute-start(bf16[12,32,512]{2,1,0:T(8,128)(2,1)S(1)} %attend_part.5.refs_0_), channel_id=1, source_target_pairs={{0,1},{1,0},{2,3},{3,2},{4,5},{5,4},{6,7},{7,6},{8,9},{9,8},{10,11... | collective-permute-start | bytes 1179656 | tf_op jit(solution)/shard_map/ppermute | solution.py:362
  83.7 15.4 %collective-permute-start.26 = (bf16[12,32,512]{2,1,0:T(8,128)(2,1)S(1)}, bf16[12,32,512]{2,1,0:T(8,128)(2,1)}, u32[]{:S(2)}, u32[]{:S(2)}) collective-permute-start(bf16[12,32,512]{2,1,0:T(8,128)(2,1)S(1)} %collective-permute-done.25.refs_2_), channel_id=1, source_target_pairs={{0,1},{1,0},{2,3},{3,2},{4,5},{5,4},{6,7},{7,6},{8,9},{9,8},{10,11... | collective-permute-start | bytes 1179656 | tf_op jit(solution)/shard_map/ppermute | solution.py:362
  92.1 6.4 %collective-permute-start.11 = (bf16[8,32,512]{2,1,0:T(8,128)(2,1)S(1)}, bf16[8,32,512]{2,1,0:T(8,128)(2,1)S(1)}, u32[]{:S(2)}, u32[]{:S(2)}) collective-permute-start(bf16[8,32,512]{2,1,0:T(8,128)(2,1)S(1)} %attend_part.3.refs_0_), channel_id=1, source_target_pairs={{0,2},{1,3},{2,0},{3,1},{4,6},{5,7},{6,4},{7,5},{8,10},{9,11},{10,... | collective-permute-start | bytes 786440 | tf_op jit(solution)/shard_map/ppermute | solution.py:362
  93.7 11.6 %collective-permute-start.17 = (bf16[12,32,512]{2,1,0:T(8,128)(2,1)S(1)}, bf16[12,32,512]{2,1,0:T(8,128)(2,1)S(1)}, u32[]{:S(2)}, u32[]{:S(2)}) collective-permute-start(bf16[12,32,512]{2,1,0:T(8,128)(2,1)S(1)} %attend_part.4.refs_0_), channel_id=1, source_target_pairs={{0,1},{1,0},{2,3},{3,2},{4,5},{5,4},{6,7},{7,6},{8,9},{9,8},{10,11... | collective-permute-start | bytes 1179656 | tf_op jit(solution)/shard_map/ppermute | solution.py:362
  93.7 11.6 %collective-permute-start.19 = (bf16[12,32,512]{2,1,0:T(8,128)(2,1)}, bf16[12,32,512]{2,1,0:T(8,128)(2,1)S(1)}, u32[]{:S(2)}, u32[]{:S(2)}) collective-permute-start(bf16[12,32,512]{2,1,0:T(8,128)(2,1)} %collective-permute-done.18.refs_2_), channel_id=1, source_target_pairs={{0,1},{1,0},{2,3},{3,2},{4,5},{5,4},{6,7},{7,6},{8,9},{9,8},{10,11... | collective-permute-start | bytes 1179656 | tf_op jit(solution)/shard_map/ppermute | solution.py:362
  98.6 10.8 %collective-permute-start.10 = (bf16[8,32,512]{2,1,0:T(8,128)(2,1)S(1)}, bf16[8,32,512]{2,1,0:T(8,128)(2,1)S(1)}, u32[]{:S(2)}, u32[]{:S(2)}) collective-permute-start(bf16[8,32,512]{2,1,0:T(8,128)(2,1)S(1)} %attend_part.3.refs_0_), channel_id=1, source_target_pairs={{0,1},{1,0},{2,3},{3,2},{4,5},{5,4},{6,7},{7,6},{8,9},{9,8},{10,11... | collective-permute-start | bytes 786440 | tf_op jit(solution)/shard_map/ppermute | solution.py:362
  98.6 10.8 %collective-permute-start.12 = (bf16[8,32,512]{2,1,0:T(8,128)(2,1)S(1)}, bf16[8,32,512]{2,1,0:T(8,128)(2,1)S(1)}, u32[]{:S(2)}, u32[]{:S(2)}) collective-permute-start(bf16[8,32,512]{2,1,0:T(8,128)(2,1)S(1)} %collective-permute-done.11.refs_2_), channel_id=1, source_target_pairs={{0,1},{1,0},{2,3},{3,2},{4,5},{5,4},{6,7},{7,6},{8,9},{9,8},{10,11... | collective-permute-start | bytes 786440 | tf_op jit(solution)/shard_map/ppermute | solution.py:362
  99.1 2.2 %copy-start = (bf16[2048,1024]{1,0:T(8,128)(2,1)S(1)}, bf16[2048,1024]{1,0:T(8,128)(2,1)}, u32[]{:S(2)}) copy-start(bf16[2048,1024]{1,0:T(8,128)(2,1)} %weight_ref.5) | copy-start | bytes 12582916
  105.3 4.1 %copy-start.1 = (bf16[2048,1024]{1,0:T(8,128)(2,1)S(1)}, bf16[2048,1024]{1,0:T(8,128)(2,1)}, u32[]{:S(2)}) copy-start(bf16[2048,1024]{1,0:T(8,128)(2,1)} %weight_ref.5) | copy-start | bytes 12582916
